TPU v7x, 128 devices: a whole 4x4x4 slice. The times are simulated.
128 devices in a mesh: row: 8 (over y, core), col: 16 (over z, x).
Axes of the slice: x: 4, y: 4, z: 4, core: 2. Of those that a mesh axis runs over, the one named last changes fastest.
Arguments:
- kernel_panel: float32 [64, 32768], P(None, ('row', 'col')), may hold values from -4 to 16, as said below
- kernel_slab: float32 [32768, 4096], P('row', 'col'), may hold values from -4 to 20, as said below
- targets: float32 [256, 32768], P(None, ('row', 'col')), may hold values from -6 to 6
Outputs:
- updated_slab: float32 [32768, 4096], P('row', 'col')
- solved_targets: float32 [256, 32768], P('col', 'row')
- panel_factor: float32 [64, 32768], P(None, ('row', 'col'))
Inputs may be any that keep to these rules, and one draw needn't show every extreme that they name: kernel_panel[:, 0:64] is symmetric and positive definite. `kernel_slab`: rows 0 to 63 equal kernel_panel[:, 32768 - 4096 : 32768]; the last 4096 rows form a symmetric matrix.
All inputs are finite; a program needn't handle non-finite values.
Results may differ from a plain program's by a relative error of at most 0.00018.
Values sent between devices are 32-bit elements; how exact they have to be, the bound alone decides.
No kernel may reach another device: no remote copies, remote signals or barrier semaphores. Data moves between devices by JAX's collectives and lax.ppermute only.
A program may use at most 64 MiB of HBM per device.

v0:
```python
import jax
import jax.numpy as jnp
from jax import lax
from jax.sharding import PartitionSpec as P


def spread(block, axis, source):
    block = jnp.where(lax.axis_index(axis) == source, block, jnp.zeros_like(block))
    return lax.psum(block, axis)


def lower_solve(factor, values):
    return jax.scipy.linalg.solve_triangular(factor, values, lower=True)


def body(kernel_panel, kernel_slab, targets):
    highest = lax.Precision.HIGHEST
    panel_width = kernel_panel.shape[0]
    row_count = lax.axis_size("row")
    row_index = lax.axis_index("row")
    flat_index = lax.axis_index(("row", "col"))
    corner_rows = jnp.concatenate([kernel_panel[:, :panel_width], targets[:, :panel_width]], 0)
    shared = spread(corner_rows, ("row", "col"), 0)
    lower_factor = jnp.linalg.cholesky(shared[:panel_width])
    panel_factor = lower_solve(lower_factor, kernel_panel)
    gathered = lax.all_gather(panel_factor, "col", axis=1, tiled=True)
    slab_factor = spread(panel_factor, "row", row_count - 1)
    product = lax.dot_general(
        gathered,
        slab_factor,
        (((0,), (0,)), ((), ())),
        precision=highest,
        preferred_element_type=jnp.float32,
    )
    update = kernel_slab - product
    head_rows = jnp.where(row_index == 0, slab_factor, update[:panel_width])
    updated_slab = jnp.concatenate([head_rows, update[panel_width:]], 0)
    solved_lead = lower_solve(lower_factor, shared[panel_width:].T).T
    result = targets - jnp.dot(
        solved_lead, panel_factor, precision=highest, preferred_element_type=jnp.float32
    )
    head_cols = jnp.where(flat_index == 0, solved_lead, result[:, :panel_width])
    result = jnp.concatenate([head_cols, result[:, panel_width:]], 1)
    solved_targets = lax.all_to_all(result, "col", split_axis=0, concat_axis=1, tiled=True)
    return (updated_slab, solved_targets, panel_factor)


def solution(mesh):
    in_specs = (P(None, ("row", "col")), P("row", "col"), P(None, ("row", "col")))
    out_specs = (P("row", "col"), P("col", "row"), P(None, ("row", "col")))
    return jax.shard_map(body, mesh=mesh, in_specs=in_specs, out_specs=out_specs, check_vma=False)
```

profile of v0, /device:TPU:0, one launch (start us, length us, event | category | flops | bytes accessed | tf_op | source)
XLA Modules:
  0.0 286.8 jit_solution(15664791899250229156)
XLA Ops:
  7.2 0.8 slice.34
  8.1 1.1 copy.17
  9.2 0.7 maximum_select_fusion
  10.0 143.3 %all-reduce.3.cloned.1.call-done = f32[320,64]{0,1:T(8,128)} async-done(((f32[320,64]{0,1:T(8,128)}), f32[320,64]{0,1:T(8,128)}) %all-reduce.3.cloned.1.call-update) | async-done | bytes 81936 | tf_op jit(solution)/shard_map/psum | solution.py:9
  153.3 0.8 slice.43
  154.1 0.8 fusion.5
  154.9 5.8 %cholesky.18 = f32[64,64]{1,0:T(8,128)S(1)} custom-call(f32[64,64]{1,0:T(8,128)S(1)} %fusion.5), custom_call_target="Cholesky" | custom-call | tf_op jit(solution)/shard_map/jit(cholesky)/cholesky | solution.py:24
  160.8 0.6 compare_reduce_fusion
  161.4 0.7 fusion.1
  162.1 4.9 %custom-call.7 = f32[1,64,64]{1,2,0:T(8,128)S(1)} custom-call(f32[1,64,64]{2,1,0:T(8,128)S(1)} %fusion.1), custom_call_target="InvertDiagBlocksLowerTriangular" | custom-call | tf_op jit(solution)/shard_map/jit(_solve_triangular)/triangular_solve | solution.py:13
  167.0 1.8 broadcast_select_fusion
  168.8 0.7 all-gather.2.cloned.1.call-update
  169.5 1.2 fusion
  170.7 1.3 convolution_subtract_fusion.1
  172.0 0.8 copy.20
  172.9 5.6 %all-to-all-start = ((f32[16,16,256]{2,1,0:T(8,128)}), f32[16,16,256]{2,1,0:T(8,128)S(1)}, u32[]{:S(2)}, u32[]{:S(2)}) async-start(f32[16,16,256]{2,1,0:T(8,128)} %bitcast.7), calls=%async_computation | async-start | bytes 524288 | tf_op jit(solution)/shard_map/all_to_all | solution.py:44
  178.5 8.7 %all-to-all-done = f32[16,16,256]{2,1,0:T(8,128)S(1)} async-done(((f32[16,16,256]{2,1,0:T(8,128)}), f32[16,16,256]{2,1,0:T(8,128)S(1)}, u32[]{:S(2)}, u32[]{:S(2)}) %all-to-all-start) | async-done | bytes 262176 | tf_op jit(solution)/shard_map/all_to_all | solution.py:44
  187.2 0.7 copy.23
  187.9 38.0 %all-reduce.5.cloned.1.call-done = f32[64,256]{1,0:T(8,128)} async-done(((f32[64,256]{1,0:T(8,128)}), f32[64,256]{1,0:T(8,128)}) %all-reduce.5.cloned.1.call-update) | async-done | bytes 65552 | tf_op jit(solution)/shard_map/psum | solution.py:9
  225.9 45.2 %all-gather.2.cloned.1.call-done = f32[64,4096]{1,0:T(8,128)} async-done(((f32[64,256]{1,0:T(8,128)}), f32[64,4096]{1,0:T(8,128)}) %all-gather.2.cloned.1.call-update) | async-done | bytes 1048592 | tf_op jit(solution)/shard_map/all_gather | solution.py:26
  271.1 6.0 %convolution_subtract_fusion = f32[4096,256]{1,0:T(8,128)S(1)} fusion(f32[4096,256]{1,0:T(8,128)} %param.6, f32[64,4096]{1,0:T(8,128)} %all-gather.2.cloned.1.call-done, f32[64,256]{1,0:T(8,128)} %all-reduce.5.cloned.1.call-done), kind=kOutput, calls=%fused_computation | convolution fusion | flops 806354944 | bytes 9502720 | tf_op jit(solution)/shard_map/dot_general | solution.py:28
  277.1 0.3 slice.45
  277.4 0.6 copy-done
  278.0 2.3 pad_maximum_fusion
  (14 shorter events, 0.4 us)
Async XLA Ops:
  7.2 146.1 %all-reduce.3.cloned.1.call-start = ((), (), s32[]{:S(2)}) async-start(), calls=%async_computation.1 | async-start | bytes 196608 | tf_op jit(solution)/shard_map/psum | solution.py:9
  9.9 216.0 %all-reduce.5.cloned.1.call-start = ((), (), s32[]{:S(2)}) async-start(), calls=%async_computation.2 | async-start | bytes 131072 | tf_op jit(solution)/shard_map/psum | solution.py:9
  168.8 102.3 %all-gather.2.cloned.1.call-start = ((), (), s32[]{:S(2)}) async-start(), calls=%async_computation.3 | async-start | bytes 1114112 | tf_op jit(solution)/shard_map/all_gather | solution.py:26
  172.9 14.3 %all-to-all-start = ((f32[16,16,256]{2,1,0:T(8,128)}), f32[16,16,256]{2,1,0:T(8,128)S(1)}, u32[]{:S(2)}, u32[]{:S(2)}) async-start(f32[16,16,256]{2,1,0:T(8,128)} %bitcast.7), calls=%async_computation | async-start | bytes 524288 | tf_op jit(solution)/shard_map/all_to_all | solution.py:44
  277.1 0.8 copy-start
Sparse Core Ops, SparseCore 0:
  13.3 139.9 all-reduce.2
  168.9 56.9 all-reduce.4
  228.6 42.4 all-gather.1
where the time goes:
time: 287 us
  waiting for transfers between devices  236 us (82%)
  other arithmetic  15.9 us (6%)
  between operations  13.9 us (5%)
  matrix products  10.2 us (4%)
  starting transfers between devices  5.75 us (2%)
  local copies, waits for them, and re-layouts  5.16 us (2%)
    psum x2, waiting for transfers between devices, spread(): return lax.psum(block, axis)  181 us
    all_gather x1, waiting for transfers between devices, body(): gathered = lax.all_gather(panel_factor, 'col', axis=1, tiled=True)  45.2 us
    all_to_all x1, waiting for transfers between devices, body(): lax.all_to_all(result, 'col', split_axis=0, concat_axis=1, tiled=True)  8.69 us
    another operation x3, other arithmetic, body(): lower_factor = jnp.linalg.cholesky(shared[:panel_width])  6.52 us
    dot_general x1, matrix products, body(): lax.dot_general(gathered, slab_factor, (((0,), (0,)), ((), ())), precisio...  6 us
  transfers between devices with their start and end apart: 4, of which 4 were waited for; matrix products, arithmetic and copies ran while one was open for 1% of the time, Pallas kernels for 0%

commit v1 on v0

--- a/solution.py
+++ b/solution.py
@@ -23,7 +23,8 @@
     shared = spread(corner_rows, ("row", "col"), 0)
     lower_factor = jnp.linalg.cholesky(shared[:panel_width])
     panel_factor = lower_solve(lower_factor, kernel_panel)
-    gathered = lax.all_gather(panel_factor, "col", axis=1, tiled=True)
+    sent = jnp.stack([panel_factor] * lax.axis_size("col"))
+    gathered = jnp.concatenate(lax.all_to_all(sent, "col", 0, 0), axis=1)
     slab_factor = spread(panel_factor, "row", row_count - 1)
     product = lax.dot_general(
         gathered,

time: 287 us -> 267 us (0.930)
  waiting for transfers between devices: 236 us -> 204 us
  blocking collectives: 0 us -> 14.1 us
    all_gather x1 -> x0, waiting for transfers between devices: 45.2 us -> none  [body(): gathered = lax.all_gather(panel_factor, 'col', axis=1, tiled=True)]
    all_to_all x0 -> x1, blocking collectives: none -> 14.1 us  [body(): lax.all_to_all(result, 'col', split_axis=0, concat_axis=1, tiled=True)]
    psum x2, waiting for transfers between devices: 181 us -> 189 us  [spread(): return lax.psum(block, axis)]
    all_to_all x1, waiting for transfers between devices: 8.69 us -> 14.4 us  [body(): gathered = jnp.concatenate(lax.all_to_all(sent, 'col', 0, 0), axis=1)]
  transfers between devices with their start and end apart: 4 -> 3, of which waited for: 4 -> 3; matrix products, arithmetic and copies ran while one was open for 1% -> 0% of each run, Pallas kernels for 0% -> 0%
where the time goes in v1:
time: 267 us
  waiting for transfers between devices  204 us (76%)
  other arithmetic  15.9 us (6%)
  between operations  14.2 us (5%)
  blocking collectives  14.1 us (5%)
  matrix products  8.66 us (3%)
  local copies, waits for them, and re-layouts  5.62 us (2%)
  starting transfers between devices  3.74 us (1%)
    psum x2, waiting for transfers between devices, spread(): return lax.psum(block, axis)  189 us
    all_to_all x1, waiting for transfers between devices, body(): gathered = jnp.concatenate(lax.all_to_all(sent, 'col', 0, 0), axis=1)  14.4 us
    all_to_all x1, blocking collectives, body(): lax.all_to_all(result, 'col', split_axis=0, concat_axis=1, tiled=True)  14.1 us
    another operation x3, other arithmetic, body(): lower_factor = jnp.linalg.cholesky(shared[:panel_width])  6.52 us
    another operation x2, other arithmetic, lower_solve(): return jax.scipy.linalg.solve_triangular(factor, values, lower=True)  5.55 us
  transfers between devices with their start and end apart: 3, of which 3 were waited for; matrix products, arithmetic and copies ran while one was open for 0% of the time, Pallas kernels for 0%

profile of v1, /device:TPU:0, one launch (start us, length us, event | category | flops | bytes accessed | tf_op | source)
XLA Modules:
  0.0 266.7 jit_solution(633331564421748093)
XLA Ops:
  7.2 0.8 slice.34
  8.1 1.1 copy.23
  9.2 0.7 maximum_select_fusion
  9.9 143.4 %all-reduce.3.cloned.1.call-done = f32[320,64]{0,1:T(8,128)} async-done(((f32[320,64]{0,1:T(8,128)}), f32[320,64]{0,1:T(8,128)}) %all-reduce.3.cloned.1.call-update) | async-done | bytes 81936 | tf_op jit(solution)/shard_map/psum | solution.py:9
  153.3 0.8 slice.43
  154.1 0.8 fusion.5
  154.9 5.8 %cholesky.18 = f32[64,64]{1,0:T(8,128)S(1)} custom-call(f32[64,64]{1,0:T(8,128)S(1)} %fusion.5), custom_call_target="Cholesky" | custom-call | tf_op jit(solution)/shard_map/jit(cholesky)/cholesky | solution.py:24
  160.8 0.6 compare_reduce_fusion
  161.4 0.7 fusion.1
  162.1 4.9 %custom-call.7 = f32[1,64,64]{1,2,0:T(8,128)S(1)} custom-call(f32[1,64,64]{2,1,0:T(8,128)S(1)} %fusion.1), custom_call_target="InvertDiagBlocksLowerTriangular" | custom-call | tf_op jit(solution)/shard_map/jit(_solve_triangular)/triangular_solve | solution.py:13
  167.0 1.7 broadcast_select_fusion
  168.7 1.2 fusion
  169.9 0.4 convolution_subtract_fusion.1
  170.6 14.1 %all_to_all.24 = f32[16,16,256]{2,1,0:T(8,128)S(1)} all-to-all(f32[16,16,256]{2,1,0:T(8,128)S(1)} %bitcast.35), channel_id=1, replica_groups=mesh['row'=8,'col'=16] {'col'}, dimensions={0} | all-to-all | bytes 524288 | tf_op jit(solution)/shard_map/all_to_all | solution.py:45
  184.7 1.1 stack.2
  185.8 3.7 %all-to-all-start = ((f32[16,64,256]{2,1,0:T(8,128)}), f32[16,64,256]{2,1,0:T(8,128)S(1)}, u32[]{:S(2)}, u32[]{:S(2)}) async-start(f32[16,64,256]{2,1,0:T(8,128)} %stack.2), calls=%async_computation | async-start | bytes 2097152 | tf_op jit(solution)/shard_map/all_to_all | solution.py:27
  189.5 0.7 all-reduce.5.cloned.1.call-update
  190.2 0.7 copy.31
  190.9 14.4 %all-to-all-done = f32[16,64,256]{2,1,0:T(8,128)S(1)} async-done(((f32[16,64,256]{2,1,0:T(8,128)}), f32[16,64,256]{2,1,0:T(8,128)S(1)}, u32[]{:S(2)}, u32[]{:S(2)}) %all-to-all-start) | async-done | bytes 1048608 | tf_op jit(solution)/shard_map/all_to_all | solution.py:27
  205.4 45.9 %all-reduce.5.cloned.1.call-done = f32[64,256]{1,0:T(8,128)} async-done(((f32[64,256]{1,0:T(8,128)}), f32[64,256]{1,0:T(8,128)}) %all-reduce.5.cloned.1.call-update) | async-done | bytes 65552 | tf_op jit(solution)/shard_map/psum | solution.py:9
  251.4 5.3 %convolution_subtract_fusion = f32[4096,256]{1,0:T(8,128)S(1)} fusion(f32[4096,256]{1,0:T(8,128)} %param.6, f32[64,4096]{1,0:T(8,128)S(1)} %bitcast.32, f32[64,256]{1,0:T(8,128)} %all-reduce.5.cloned.1.call-done), kind=kOutput, calls=%fused_computation | convolution fusion | flops 806354944 | bytes 9502720 | tf_op jit(solution)/shard_map/dot_general | solution.py:29
  256.7 0.3 slice.45
  257.0 0.6 copy-done.1
  257.5 2.3 pad_maximum_fusion
  (16 shorter events, 0.6 us)
Async XLA Ops:
  7.2 146.1 %all-reduce.3.cloned.1.call-start = ((), (), s32[]{:S(2)}) async-start(), calls=%async_computation.2 | async-start | bytes 196608 | tf_op jit(solution)/shard_map/psum | solution.py:9
  168.7 36.7 %copy-start = (f32[64,256]{1,0:T(8,128)}, f32[64,256]{1,0:T(8,128)S(1)}, u32[]{:S(2)}) copy-start(f32[64,256]{1,0:T(8,128)S(1)} %get-tuple-element.5) | copy-start | bytes 196612
  185.8 19.5 %all-to-all-start = ((f32[16,64,256]{2,1,0:T(8,128)}), f32[16,64,256]{2,1,0:T(8,128)S(1)}, u32[]{:S(2)}, u32[]{:S(2)}) async-start(f32[16,64,256]{2,1,0:T(8,128)} %stack.2), calls=%async_computation | async-start | bytes 2097152 | tf_op jit(solution)/shard_map/all_to_all | solution.py:27
  189.4 61.9 %all-reduce.5.cloned.1.call-start = ((), (), s32[]{:S(2)}) async-start(), calls=%async_computation.3 | async-start | bytes 131072 | tf_op jit(solution)/shard_map/psum | solution.py:9
  256.7 0.8 copy-start.1
Sparse Core Ops, SparseCore 0:
  13.3 139.9 all-reduce.2
  192.7 58.6 all-reduce.4
